TPU v7x, 512 devices: a whole 4x4x16 slice. The times are simulated.
512 devices in a mesh: tm: 16 (over y, x_lo, core), expert: 32 (over x_hi, z).
Axes of the slice: x: 4 (x_hi: 2, x_lo: 2; x = x_hi * 2 + x_lo), y: 4, z: 16, core: 2. Of those that a mesh axis runs over, the one named last changes fastest.
Arguments:
- latents: bfloat16 [32, 2048, 1024], P('expert', 'tm'), may hold values from -16 to 16
- queries: bfloat16 [32, 2048, 1024], P('expert', 'tm'), may hold values from -6 to 6
- keys: bfloat16 [32, 2048, 1024], P('expert', 'tm'), may hold values from -6 to 6
- values: bfloat16 [32, 2048, 1024], P('expert', 'tm'), may hold values from -8 to 8
- inpaint_mask: int32 [32, 2048], P('expert', 'tm'), may hold values 0 or 1
- key_bias: bfloat16 [16], replicated, may hold values from -3 to 3
- out_weight: bfloat16 [1024, 1024], replicated, may hold values from -0.1875 to 0.1875
- modulation: float32 [32, 2, 1024], P('expert'), may hold values from -3 to 3
- branch_gates: float32 [32, 2, 1024], P('expert'), may hold values from 0.5 to 1.5
- expert_ids: int32 [32, 2048, 2], P('expert', 'tm'), may hold values from 0 to 31, as said below
- gate_values: float32 [32, 2048, 2], P('expert', 'tm'), may hold values from 0.2 to 1
- up_weight: bfloat16 [32, 1024, 1024], P('expert', None, 'tm'), may hold values from -0.1875 to 0.1875
- down_weight: bfloat16 [32, 1024, 1024], P('expert', 'tm'), may hold values from -0.1875 to 0.1875
Outputs:
- layer_out: bfloat16 [32, 2048, 1024], P('expert', 'tm')
Inputs may be any that keep to these rules, and one draw needn't show every extreme that they name: `expert_ids`: A token's two ids differ. Within each device's block of 128 positions of one clip, no id is named more than 16 times, and one id is named exactly 16 times; that id is the same for all clips at the same block position.
All inputs are finite; a program needn't handle non-finite values. No bound on the sum of `inpaint_mask` on one device may be relied on, other than what follows from the above.
Results may differ from a plain program's by a relative error of at most 0.01.
Values may be sent and summed in bfloat16 or wider, within the bound.
A program may use at most 128 MiB of HBM per device.

v0:
```python
import jax
import jax.numpy as jnp
from jax import lax
from jax.sharding import PartitionSpec as P

eps = 1e-06
query_block = 512


def head_attention(query_rows, key_rows, value_rows, offset_row):
    outputs = []
    for first in range(0, query_rows.shape[0], query_block):
        block = query_rows[first : first + query_block]
        scores = (
            jnp.dot(block, key_rows.T, preferred_element_type=jnp.float32) + offset_row[None, :]
        )
        highest = jnp.max(scores, axis=1, keepdims=True)
        unscaled = jnp.exp(scores - highest)
        total = jnp.sum(unscaled, axis=1, keepdims=True)
        weighted = jnp.dot(
            unscaled.astype(jnp.bfloat16), value_rows, preferred_element_type=jnp.float32
        )
        outputs.append((weighted / total).astype(jnp.bfloat16))
    return jnp.concatenate(outputs, axis=0)


def layer_norm(mixed, shift_row, scale_row):
    center = jnp.mean(mixed, axis=-1, keepdims=True)
    deviation = mixed - center
    variance = jnp.mean(deviation * deviation, axis=-1, keepdims=True)
    return deviation * lax.rsqrt(variance + eps) * (1.0 + scale_row) + shift_row


def on_device(
    latents,
    queries,
    keys,
    values,
    inpaint_mask,
    key_bias,
    out_weight,
    modulation,
    branch_gates,
    expert_ids,
    gate_values,
    up_weight,
    down_weight,
):
    tok_rows = latents.shape[1]
    model_width = latents.shape[2]
    head_count = key_bias.shape[0]
    head_width = model_width // head_count
    score_scale = head_width ** (-0.5)
    full_up, full_down = (
        lax.all_gather(up_weight, "tm", axis=2, tiled=True),
        lax.all_gather(down_weight, "tm", axis=1, tiled=True),
    )
    scaled_queries = queries[0] * jnp.asarray(score_scale, jnp.bfloat16)
    offsets = jnp.where(
        inpaint_mask[0][:, None] == 1, key_bias[None, :], jnp.zeros((), jnp.bfloat16)
    )
    offset_cols = (
        jnp.zeros((tok_rows, head_count, head_width), jnp.bfloat16).at[:, :, 0].set(offsets)
    )
    packed = jnp.concatenate(
        [
            scaled_queries.reshape(tok_rows, head_count, head_width),
            keys[0].reshape(tok_rows, head_count, head_width),
            values[0].reshape(tok_rows, head_count, head_width),
            offset_cols,
        ],
        axis=2,
    )
    packed = jnp.transpose(packed, (1, 0, 2))
    gathered = lax.all_to_all(packed, "tm", split_axis=0, concat_axis=0, tiled=True)
    clip_rows = gathered.reshape(-1, 4 * head_width)
    head_out = head_attention(
        clip_rows[:, :head_width],
        clip_rows[:, head_width : 2 * head_width],
        clip_rows[:, 2 * head_width : 3 * head_width],
        clip_rows[:, 3 * head_width].astype(jnp.float32),
    )
    head_out = head_out.reshape(head_count, tok_rows, head_width)
    attended_heads = lax.all_to_all(head_out, "tm", split_axis=0, concat_axis=0, tiled=True)
    projected = jnp.einsum(
        "hid,hdo->io",
        attended_heads,
        out_weight.reshape(head_count, head_width, model_width),
        preferred_element_type=jnp.float32,
    )
    mixed = latents[0].astype(jnp.float32) + branch_gates[0, 0][None, :] * projected
    normed = layer_norm(mixed, modulation[0, 0][None, :], modulation[0, 1][None, :]).astype(
        jnp.bfloat16
    )
    local_experts = up_weight.shape[0]
    source_count = lax.axis_size("expert")
    expert_count = local_experts * source_count
    capacity = 4 * tok_rows // expert_count
    choice_list = expert_ids[0].reshape(2 * tok_rows)
    hits = (choice_list[:, None] == jnp.arange(expert_count, dtype=jnp.int32)[None, :]).astype(
        jnp.int32
    )
    ranks = jnp.sum((jnp.cumsum(hits, axis=0) - 1) * hits, axis=1)
    target = ranks * expert_count + choice_list
    placing = (
        jnp.arange(capacity * expert_count, dtype=jnp.int32)[:, None] == target[None, :]
    ).astype(jnp.bfloat16)
    doubled = jnp.repeat(normed, 2, axis=0)
    slots = jnp.dot(placing, doubled, preferred_element_type=jnp.float32).astype(jnp.bfloat16)
    slots = slots.reshape(capacity, expert_count, model_width)
    arrived = lax.all_to_all(slots, "expert", split_axis=1, concat_axis=1, tiled=True)
    slot_count = arrived.shape[0]
    grouped = arrived.reshape(slot_count, source_count, local_experts, model_width)
    hidden = jax.nn.gelu(
        jnp.einsum("csed,edf->csef", grouped, full_up, preferred_element_type=jnp.float32),
        approximate=True,
    ).astype(jnp.bfloat16)
    produced = jnp.einsum(
        "csef,efd->csed", hidden, full_down, preferred_element_type=jnp.float32
    ).astype(jnp.bfloat16)
    produced = produced.reshape(slot_count, source_count * local_experts, model_width)
    returned = lax.all_to_all(produced, "expert", split_axis=1, concat_axis=1, tiled=True)
    picked = jnp.einsum(
        "sa,sd->ad",
        placing,
        returned.reshape(capacity * expert_count, model_width),
        preferred_element_type=jnp.float32,
    )
    picked = picked.reshape(tok_rows, 2, model_width)
    combined = jnp.sum(gate_values[0][:, :, None] * picked, axis=1)
    layer_out = (mixed + branch_gates[0, 1][None, :] * combined).astype(jnp.bfloat16)
    return layer_out[None]


def solution(mesh):
    placed = (
        P("expert", "tm", None),
        P("expert", "tm", None),
        P("expert", "tm", None),
        P("expert", "tm", None),
        P("expert", "tm"),
        P(),
        P(),
        P("expert", None, None),
        P("expert", None, None),
        P("expert", "tm", None),
        P("expert", "tm", None),
        P("expert", None, "tm"),
        P("expert", "tm", None),
    )
    return jax.shard_map(
        on_device, mesh=mesh, in_specs=placed, out_specs=P("expert", "tm", None), check_vma=False
    )
```

profile of v0, /device:TPU:32, one launch (start us, length us, event | category | flops | bytes accessed | tf_op | source)
XLA Modules:
  0.0 219.5 jit_solution(16701565516031589247)
XLA Ops:
  6.5 0.0 copy-start
  6.5 0.0 copy-start.4
  6.5 0.0 copy-start.2
  6.5 1.3 copy.26
  7.8 1.1 copy.27
  9.0 1.1 copy.28
  10.1 0.7 compare_bitcast_fusion
  10.8 0.7 broadcast_select_fusion
  11.5 1.1 fusion.65
  12.6 5.6 %all-to-all-start = ((bf16[16,128,256]{1,2,0:T(8,128)(2,1)}), bf16[16,128,256]{1,2,0:T(8,128)(2,1)}, u32[]{:S(2)}, u32[]{:S(2)}) async-start(bf16[16,128,256]{1,2,0:T(8,128)(2,1)} %fusion.65), calls=%async_computation | async-start | bytes 2097152 | tf_op jit(solution)/shard_map/all_to_all | solution.py:75
  18.2 0.0 all-gather.3.cloned.1.call-start
  18.2 0.7 all-gather.3.cloned.1.call-update
  18.9 0.0 copy-done.4
  18.9 0.1 copy.31
  19.0 0.1 eq.75
  19.2 0.1 eq.71
  19.3 0.6 reduce-window.6
  19.9 0.2 slice_reduce_fusion
  20.2 0.1 fusion.91
  20.3 0.0 copy-done.2
  20.3 14.5 %all-to-all-done = bf16[16,128,256]{1,2,0:T(8,128)(2,1)} async-done(((bf16[16,128,256]{1,2,0:T(8,128)(2,1)}), bf16[16,128,256]{1,2,0:T(8,128)(2,1)}, u32[]{:S(2)}, u32[]{:S(2)}) %all-to-all-start) | async-done | bytes 1048608 | tf_op jit(solution)/shard_map/all_to_all | solution.py:75
  34.8 1.5 copy.29
  36.3 0.4 convert_reduce_fusion
  36.7 0.8 fusion.76
  37.5 0.8 fusion.78
  38.3 0.9 add_reduce_fusion.3
  39.2 2.1 fusion
  41.3 1.0 fusion.43
  42.2 2.5 %fusion.2 = (f32[512]{0:T(512)S(1)}, f32[512]{0:T(512)S(1)}, f32[512]{0:T(512)S(1)}) fusion(f32[512,2048]{1,0:T(8,128)S(1)} %get-tuple-element.30, f32[512]{0:T(512)S(1)} %get-tuple-element.18, f32[2048]{0:T(1024)S(1)} %convert_reduce_fusion, f32[512]{0:T(512)S(1)} %get-tuple-element.19, f32[512,2048]{1,0:T(8,128)S(1)} %fusion.78, ...), kind=kLoop, calls=%fused_computation.10 | loop fusion | flops 9435648 | bytes 12603392 | tf_op jit(solution)/shard_map/reduce_sum | solution.py:19
  44.7 1.0 fusion.49
  45.7 1.0 fusion.55
  46.6 0.0 copy-start.3
  46.6 0.0 copy-start.1
  46.7 1.0 fusion.61
  47.6 0.8 copy_bitcast_fusion
  48.4 3.7 %all-to-all-start.1 = ((bf16[16,128,64]{1,2,0:T(8,128)(2,1)}), bf16[16,128,64]{1,2,0:T(8,128)(2,1)S(1)}, u32[]{:S(2)}, u32[]{:S(2)}) async-start(bf16[16,128,64]{1,2,0:T(8,128)(2,1)} %copy_bitcast_fusion), calls=%async_computation.1 | async-start | bytes 524288 | tf_op jit(solution)/shard_map/all_to_all | solution.py:84
  52.1 0.0 copy-done.3
  52.2 9.1 %all-to-all-done.1 = bf16[16,128,64]{1,2,0:T(8,128)(2,1)S(1)} async-done(((bf16[16,128,64]{1,2,0:T(8,128)(2,1)}), bf16[16,128,64]{1,2,0:T(8,128)(2,1)S(1)}, u32[]{:S(2)}, u32[]{:S(2)}) %all-to-all-start.1) | async-done | bytes 262176 | tf_op jit(solution)/shard_map/all_to_all | solution.py:84
  61.3 0.0 copy-done
  61.3 0.0 copy-done.1
  61.3 0.5 fusion.98
  61.8 0.2 multiply_reduce_fusion
  62.0 0.2 add_convert_fusion.1
  62.2 0.3 broadcast_in_dim.27
  62.5 1.0 reshape.208
  63.5 1.5 convolution_convert_fusion
  65.0 1.6 copy.34
  66.6 17.5 %all-to-all-start.2 = ((bf16[16,32,1024]{2,0,1:T(8,128)(2,1)}), bf16[16,32,1024]{2,0,1:T(8,128)(2,1)}, u32[]{:S(2)}, u32[]{:S(2)}) async-start(bf16[16,32,1024]{2,0,1:T(8,128)(2,1)} %copy.34), calls=%async_computation.2 | async-start | bytes 2097152 | tf_op jit(solution)/shard_map/all_to_all | solution.py:111
  84.0 0.0 all-gather.5.cloned.1.call-start
  84.1 0.7 all-gather.5.cloned.1.call-update
  84.8 0.0 all-gather.3.cloned.1.call-done
  84.8 43.0 %all-gather.5.cloned.1.call-done = bf16[1,1024,1024]{2,1,0:T(8,128)(2,1)} async-done(((bf16[1,64,1024]{2,1,0:T(8,128)(2,1)}), bf16[1,1024,1024]{2,1,0:T(8,128)(2,1)}) %all-gather.5.cloned.1.call-update) | async-done | bytes 2097168 | tf_op jit(solution)/shard_map/all_gather | solution.py:56
  127.8 12.3 %all-to-all-done.2 = bf16[16,32,1024]{2,0,1:T(8,128)(2,1)} async-done(((bf16[16,32,1024]{2,0,1:T(8,128)(2,1)}), bf16[16,32,1024]{2,0,1:T(8,128)(2,1)}, u32[]{:S(2)}, u32[]{:S(2)}) %all-to-all-start.2) | async-done | bytes 1048608 | tf_op jit(solution)/shard_map/all_to_all | solution.py:111
  140.1 6.2 %fusion.31 = bf16[16,32,1024]{2,1,0:T(8,128)(2,1)} fusion(bf16[1,1024,1024]{2,1,0:T(8,128)(2,1)} %all-gather.5.cloned.1.call-done, bf16[1,1024,1024]{1,2,0:T(8,128)(2,1)} %all-gather.3.cloned.1.call-done, bf16[16,32,1024]{2,0,1:T(8,128)(2,1)} %all-to-all-done.2), kind=kOutput, calls=%fused_computation.35 | convolution fusion | flops 2152726528 | bytes 6291456 | tf_op jit(solution)/shard_map/csef,efd->csed/dot_general | solution.py:118
  146.3 0.0 copy-start.5
  146.3 2.8 %copy.37 = bf16[16,32,1024]{2,0,1:T(8,128)(2,1)} copy(bf16[16,32,1024]{2,1,0:T(8,128)(2,1)} %fusion.31) | data formatting | bytes 2097152 | tf_op jit(solution)/shard_map/convert_element_type | solution.py:120
  149.1 4.5 %all-to-all-start.3 = ((bf16[16,32,1024]{2,0,1:T(8,128)(2,1)}), bf16[16,32,1024]{2,0,1:T(8,128)(2,1)}, u32[]{:S(2)}, u32[]{:S(2)}) async-start(bf16[16,32,1024]{2,0,1:T(8,128)(2,1)} %copy.37), calls=%async_computation.3 | async-start | bytes 2097152 | tf_op jit(solution)/shard_map/all_to_all | solution.py:122
  153.6 0.1 iota_compare_fusion.2
  153.8 0.2 eq.81
  154.0 55.7 %all-to-all-done.3 = bf16[16,32,1024]{2,0,1:T(8,128)(2,1)} async-done(((bf16[16,32,1024]{2,0,1:T(8,128)(2,1)}), bf16[16,32,1024]{2,0,1:T(8,128)(2,1)}, u32[]{:S(2)}, u32[]{:S(2)}) %all-to-all-start.3) | async-done | bytes 1048608 | tf_op jit(solution)/shard_map/all_to_all | solution.py:122
  209.7 1.8 copy.38
  211.5 0.0 copy-done.5
  211.5 0.4 fusion.37
  211.9 0.8 fusion.84
  (9 shorter events, 0.1 us)
Async XLA Ops:
  6.5 54.7 %copy-start = (bf16[1024,1024]{1,0:T(8,128)(2,1)S(1)}, bf16[1024,1024]{1,0:T(8,128)(2,1)}, u32[]{:S(2)}) copy-start(bf16[1024,1024]{1,0:T(8,128)(2,1)} %param.21) | copy-start | bytes 6291460
  6.5 12.4 %copy-start.4 = (s32[1,128,2]{1,2,0:T(2,128)S(1)}, s32[1,128,2]{1,2,0:T(2,128)}, u32[]{:S(2)}) copy-start(s32[1,128,2]{1,2,0:T(2,128)} %param.24) | copy-start | bytes 3076
  6.5 13.7 %copy-start.2 = (f32[1,2,1024]{2,1,0:T(2,128)S(1)}, f32[1,2,1024]{2,1,0:T(2,128)}, u32[]{:S(2)}) copy-start(f32[1,2,1024]{2,1,0:T(2,128)} %param.23) | copy-start | bytes 24580
  12.6 22.2 %all-to-all-start = ((bf16[16,128,256]{1,2,0:T(8,128)(2,1)}), bf16[16,128,256]{1,2,0:T(8,128)(2,1)}, u32[]{:S(2)}, u32[]{:S(2)}) async-start(bf16[16,128,256]{1,2,0:T(8,128)(2,1)} %fusion.65), calls=%async_computation | async-start | bytes 2097152 | tf_op jit(solution)/shard_map/all_to_all | solution.py:75
  18.2 66.6 %all-gather.3.cloned.1.call-start = ((), (), s32[]{:S(2)}) async-start(), calls=%async_computation.4 | async-start | bytes 2228224 | tf_op jit(solution)/shard_map/all_gather | solution.py:55
  46.6 5.5 %copy-start.3 = (f32[1,2,1024]{2,1,0:T(2,128)S(1)}, f32[1,2,1024]{2,1,0:T(2,128)}, u32[]{:S(2)}) copy-start(f32[1,2,1024]{2,1,0:T(2,128)} %param.22) | copy-start | bytes 24580
  46.6 14.6 %copy-start.1 = (bf16[1,128,1024]{2,1,0:T(8,128)(2,1)S(1)}, bf16[1,128,1024]{2,1,0:T(8,128)(2,1)}, u32[]{:S(2)}) copy-start(bf16[1,128,1024]{2,1,0:T(8,128)(2,1)} %param.15) | copy-start | bytes 786436
  48.4 12.9 %all-to-all-start.1 = ((bf16[16,128,64]{1,2,0:T(8,128)(2,1)}), bf16[16,128,64]{1,2,0:T(8,128)(2,1)S(1)}, u32[]{:S(2)}, u32[]{:S(2)}) async-start(bf16[16,128,64]{1,2,0:T(8,128)(2,1)} %copy_bitcast_fusion), calls=%async_computation.1 | async-start | bytes 524288 | tf_op jit(solution)/shard_map/all_to_all | solution.py:84
  66.6 73.5 %all-to-all-start.2 = ((bf16[16,32,1024]{2,0,1:T(8,128)(2,1)}), bf16[16,32,1024]{2,0,1:T(8,128)(2,1)}, u32[]{:S(2)}, u32[]{:S(2)}) async-start(bf16[16,32,1024]{2,0,1:T(8,128)(2,1)} %copy.34), calls=%async_computation.2 | async-start | bytes 2097152 | tf_op jit(solution)/shard_map/all_to_all | solution.py:111
  84.0 43.8 %all-gather.5.cloned.1.call-start = ((), (), s32[]{:S(2)}) async-start(), calls=%async_computation.5 | async-start | bytes 2228224 | tf_op jit(solution)/shard_map/all_gather | solution.py:56
  146.3 65.1 %copy-start.5 = (f32[1,128,2]{1,2,0:T(2,128)S(1)}, f32[1,128,2]{1,2,0:T(2,128)}, u32[]{:S(2)}) copy-start(f32[1,128,2]{1,2,0:T(2,128)} %param.25) | copy-start | bytes 3076
  149.1 60.5 %all-to-all-start.3 = ((bf16[16,32,1024]{2,0,1:T(8,128)(2,1)}), bf16[16,32,1024]{2,0,1:T(8,128)(2,1)}, u32[]{:S(2)}, u32[]{:S(2)}) async-start(bf16[16,32,1024]{2,0,1:T(8,128)(2,1)} %copy.37), calls=%async_computation.3 | async-start | bytes 2097152 | tf_op jit(solution)/shard_map/all_to_all | solution.py:122
Sparse Core Ops, SparseCore 0:
  21.2 47.8 all-gather.2
  87.0 40.7 all-gather.4
where the time goes:
time: 220 us
  waiting for transfers between devices  136 us (62%)
  starting transfers between devices  31.3 us (14%)
  matrix products  17 us (8%)
  between operations  13.7 us (6%)
  local copies, waits for them, and re-layouts  13.2 us (6%)
  other arithmetic  8.24 us (4%)
    all_to_all x1, waiting for transfers between devices, on_device(): lax.all_to_all(produced, 'expert', split_axis=1, concat_axis=1, tiled=True)  55.7 us
    all_gather x1, waiting for transfers between devices, on_device(): lax.all_gather(down_weight, 'tm', axis=1, tiled=True)  43 us
    all_to_all x1, starting transfers between devices, on_device(): lax.all_to_all(slots, 'expert', split_axis=1, concat_axis=1, tiled=True)  17.5 us
    all_to_all x1, waiting for transfers between devices, on_device(): lax.all_to_all(packed, 'tm', split_axis=0, concat_axis=0, tiled=True)  14.5 us
    all_to_all x1, waiting for transfers between devices, on_device(): lax.all_to_all(slots, 'expert', split_axis=1, concat_axis=1, tiled=True)  12.3 us
    all_to_all x1, waiting for transfers between devices, on_device(): lax.all_to_all(head_out, 'tm', split_axis=0, concat_axis=0, tiled=True)  9.1 us
    dot_general x1, matrix products, on_device(): jnp.einsum('csef,efd->csed', hidden, full_down, preferred_element_type=jn...  6.21 us
    all_to_all x1, starting transfers between devices, on_device(): lax.all_to_all(packed, 'tm', split_axis=0, concat_axis=0, tiled=True)  5.55 us
  transfers between devices with their start and end apart: 6, of which 5 were waited for; matrix products, arithmetic and copies ran while one was open for 9% of the time, Pallas kernels for 0%

commit v1 on v0

--- a/solution.py
+++ b/solution.py
@@ -53,7 +53,9 @@
     score_scale = head_width ** (-0.5)
     full_up, full_down = (
         lax.all_gather(up_weight, "tm", axis=2, tiled=True),
-        lax.all_gather(down_weight, "tm", axis=1, tiled=True),
+        jnp.concatenate(
+            lax.all_to_all(jnp.stack([down_weight] * lax.axis_size("tm")), "tm", 0, 0), axis=1
+        ),
     )
     scaled_queries = queries[0] * jnp.asarray(score_scale, jnp.bfloat16)
     offsets = jnp.where(

time: 220 us -> 248 us (1.13)
  waiting for transfers between devices: 136 us -> 157 us
  starting transfers between devices: 31.3 us -> 35.8 us
    all_gather x1, waiting for transfers between devices: 0.02 us -> 43.9 us  [on_device(): lax.all_gather(up_weight, 'tm', axis=2, tiled=True)]
    all_gather x1 -> x0, waiting for transfers between devices: 43 us -> none  [on_device(): lax.all_gather(down_weight, 'tm', axis=1, tiled=True)]
    all_to_all x0 -> x1, waiting for transfers between devices: none -> 22.3 us  [on_device(): lax.all_to_all(jnp.stack([down_weight] * lax.axis_size('tm')), 'tm', 0, 0)]
    all_to_all x0 -> x1, starting transfers between devices: none -> 4.6 us  [on_device(): lax.all_to_all(jnp.stack([down_weight] * lax.axis_size('tm')), 'tm', 0, 0)]
  transfers between devices with their start and end apart: 6 -> 6, of which waited for: 5 -> 6; matrix products, arithmetic and copies ran while one was open for 9% -> 3% of each run, Pallas kernels for 0% -> 0%
where the time goes in v1:
time: 248 us; the launch traced here: 247 us
  waiting for transfers between devices  157 us (63%)
  starting transfers between devices  35.8 us (14%)
  matrix products  17 us (7%)
  local copies, waits for them, and re-layouts  14.8 us (6%)
  between operations  13.7 us (6%)
  other arithmetic  8.3 us (3%)
    all_to_all x1, waiting for transfers between devices, on_device(): lax.all_to_all(produced, 'expert', split_axis=1, concat_axis=1, tiled=True)  55.9 us
    all_gather x1, waiting for transfers between devices, on_device(): lax.all_gather(up_weight, 'tm', axis=2, tiled=True)  43.9 us
    all_to_all x1, waiting for transfers between devices, on_device(): lax.all_to_all(jnp.stack([down_weight] * lax.axis_size('tm')), 'tm', 0, 0)  22.3 us
    all_to_all x1, starting transfers between devices, on_device(): lax.all_to_all(slots, 'expert', split_axis=1, concat_axis=1, tiled=True)  17.6 us
    all_to_all x1, waiting for transfers between devices, on_device(): lax.all_to_all(packed, 'tm', split_axis=0, concat_axis=0, tiled=True)  16.4 us
    all_to_all x1, waiting for transfers between devices, on_device(): lax.all_to_all(slots, 'expert', split_axis=1, concat_axis=1, tiled=True)  11.3 us
    all_to_all x1, waiting for transfers between devices, on_device(): lax.all_to_all(head_out, 'tm', split_axis=0, concat_axis=0, tiled=True)  6.94 us
    dot_general x1, matrix products, on_device(): jnp.einsum('csef,efd->csed', hidden, full_down, preferred_element_type=jn...  6.22 us
  transfers between devices with their start and end apart: 6, of which 6 were waited for; matrix products, arithmetic and copies ran while one was open for 3% of the time, Pallas kernels for 0%

profile of v1, /device:TPU:32, one launch (start us, length us, event | category | flops | bytes accessed | tf_op | source)
XLA Modules:
  0.0 247.1 jit_solution(16946836829553721731)
XLA Ops:
  6.5 0.0 copy-start
  6.5 1.3 copy.26
  7.9 1.1 copy.27
  9.0 1.1 copy.28
  10.1 0.7 compare_bitcast_fusion
  10.8 0.7 broadcast_select_fusion
  11.5 1.2 fusion.60
  12.7 5.6 %all-to-all-start = ((bf16[16,128,256]{1,2,0:T(8,128)(2,1)}), bf16[16,128,256]{1,2,0:T(8,128)(2,1)}, u32[]{:S(2)}, u32[]{:S(2)}) async-start(bf16[16,128,256]{1,2,0:T(8,128)(2,1)} %fusion.60), calls=%async_computation | async-start | bytes 2097152 | tf_op jit(solution)/shard_map/all_to_all | solution.py:77
  18.2 0.0 copy-done.5
  18.3 0.1 copy.31
  18.4 0.1 eq.75
  18.5 16.4 %all-to-all-done = bf16[16,128,256]{1,2,0:T(8,128)(2,1)} async-done(((bf16[16,128,256]{1,2,0:T(8,128)(2,1)}), bf16[16,128,256]{1,2,0:T(8,128)(2,1)}, u32[]{:S(2)}, u32[]{:S(2)}) %all-to-all-start) | async-done | bytes 1048608 | tf_op jit(solution)/shard_map/all_to_all | solution.py:77
  34.9 1.5 copy.29
  36.4 0.4 convert_reduce_fusion
  36.8 0.8 fusion.71
  37.6 0.8 fusion.73
  38.4 0.9 add_reduce_fusion.3
  39.2 2.1 fusion
  41.3 1.0 fusion.38
  42.3 2.5 %fusion.2 = (f32[512]{0:T(512)S(1)}, f32[512]{0:T(512)S(1)}, f32[512]{0:T(512)S(1)}) fusion(f32[512,2048]{1,0:T(8,128)S(1)} %get-tuple-element.30, f32[512]{0:T(512)S(1)} %get-tuple-element.18, f32[2048]{0:T(1024)S(1)} %convert_reduce_fusion, f32[512]{0:T(512)S(1)} %get-tuple-element.19, f32[512,2048]{1,0:T(8,128)S(1)} %fusion.73, ...), kind=kLoop, calls=%fused_computation.10 | loop fusion | flops 9435648 | bytes 12603392 | tf_op jit(solution)/shard_map/reduce_sum | solution.py:19
  44.8 1.0 fusion.44
  45.7 1.0 fusion.50
  46.7 0.0 copy-start.2
  46.7 1.0 fusion.56
  47.7 0.0 copy-start.3
  47.7 0.0 copy-start.4
  47.7 0.0 copy-start.1
  47.7 0.8 copy_bitcast_fusion
  48.5 3.5 %all-to-all-start.1 = ((bf16[16,128,64]{1,2,0:T(8,128)(2,1)}), bf16[16,128,64]{1,2,0:T(8,128)(2,1)S(1)}, u32[]{:S(2)}, u32[]{:S(2)}) async-start(bf16[16,128,64]{1,2,0:T(8,128)(2,1)} %copy_bitcast_fusion), calls=%async_computation.1 | async-start | bytes 524288 | tf_op jit(solution)/shard_map/all_to_all | solution.py:86
  52.0 0.1 eq.71
  52.2 0.6 reduce-window.6
  52.8 0.2 slice_reduce_fusion
  53.0 0.1 fusion.86
  53.1 6.9 %all-to-all-done.1 = bf16[16,128,64]{1,2,0:T(8,128)(2,1)S(1)} async-done(((bf16[16,128,64]{1,2,0:T(8,128)(2,1)}), bf16[16,128,64]{1,2,0:T(8,128)(2,1)S(1)}, u32[]{:S(2)}, u32[]{:S(2)}) %all-to-all-start.1) | async-done | bytes 262176 | tf_op jit(solution)/shard_map/all_to_all | solution.py:86
  60.0 0.0 copy-done.2
  60.0 1.6 stack.2
  61.6 4.6 %all-to-all-start.3 = ((bf16[16,1,64,1024]{3,2,1,0:T(8,128)(2,1)}), bf16[16,1,64,1024]{3,2,1,0:T(8,128)(2,1)}, u32[]{:S(2)}, u32[]{:S(2)}) async-start(bf16[16,1,64,1024]{3,2,1,0:T(8,128)(2,1)} %stack.2), calls=%async_computation.3 | async-start | bytes 4194304 | tf_op jit(solution)/shard_map/all_to_all | solution.py:57
  66.2 0.0 copy-done.3
  66.2 0.0 copy-done.4
  66.3 0.0 copy-done
  66.3 0.0 copy-done.1
  66.3 0.6 fusion.93
  66.8 0.2 multiply_reduce_fusion
  67.1 0.2 add_convert_fusion.1
  67.2 0.3 broadcast_in_dim.27
  67.5 1.0 reshape.213
  68.5 1.5 convolution_convert_fusion.1
  70.0 1.6 copy.34
  71.6 22.3 %all-to-all-done.3 = bf16[16,1,64,1024]{3,2,1,0:T(8,128)(2,1)} async-done(((bf16[16,1,64,1024]{3,2,1,0:T(8,128)(2,1)}), bf16[16,1,64,1024]{3,2,1,0:T(8,128)(2,1)}, u32[]{:S(2)}, u32[]{:S(2)}) %all-to-all-start.3) | async-done | bytes 2097184 | tf_op jit(solution)/shard_map/all_to_all | solution.py:57
  93.9 17.6 %all-to-all-start.2 = ((bf16[16,32,1024]{2,0,1:T(8,128)(2,1)}), bf16[16,32,1024]{2,0,1:T(8,128)(2,1)}, u32[]{:S(2)}, u32[]{:S(2)}) async-start(bf16[16,32,1024]{2,0,1:T(8,128)(2,1)} %copy.34), calls=%async_computation.2 | async-start | bytes 2097152 | tf_op jit(solution)/shard_map/all_to_all | solution.py:113
  111.5 0.0 all-gather.2.cloned.1.call-start
  111.6 0.7 all-gather.2.cloned.1.call-update
  112.2 43.9 %all-gather.2.cloned.1.call-done = bf16[1,1024,1024]{1,2,0:T(8,128)(2,1)} async-done(((bf16[1,1024,64]{1,2,0:T(8,128)(2,1)}), bf16[1,1024,1024]{1,2,0:T(8,128)(2,1)}) %all-gather.2.cloned.1.call-update) | async-done | bytes 2097168 | tf_op jit(solution)/shard_map/all_gather | solution.py:55
  156.2 11.3 %all-to-all-done.2 = bf16[16,32,1024]{2,0,1:T(8,128)(2,1)} async-done(((bf16[16,32,1024]{2,0,1:T(8,128)(2,1)}), bf16[16,32,1024]{2,0,1:T(8,128)(2,1)}, u32[]{:S(2)}, u32[]{:S(2)}) %all-to-all-start.2) | async-done | bytes 1048608 | tf_op jit(solution)/shard_map/all_to_all | solution.py:113
  167.5 6.2 %convolution_convert_fusion = bf16[16,32,1024]{2,1,0:T(8,128)(2,1)} fusion(bf16[1024,1024,1]{1,0,2:T(8,128)(2,1)} %bitcast.26, bf16[1,1024,1024]{1,2,0:T(8,128)(2,1)} %all-gather.2.cloned.1.call-done, bf16[16,32,1024]{2,0,1:T(8,128)(2,1)} %all-to-all-done.2), kind=kOutput, calls=%fused_computation.33 | convolution fusion | flops 2152726528 | bytes 6291456 | tf_op jit(solution)/shard_map/csef,efd->csed/dot_general | solution.py:120
  173.7 2.8 %copy.37 = bf16[16,32,1024]{2,0,1:T(8,128)(2,1)} copy(bf16[16,32,1024]{2,1,0:T(8,128)(2,1)} %convolution_convert_fusion) | data formatting | bytes 2097152 | tf_op jit(solution)/shard_map/convert_element_type | solution.py:122
  176.5 4.5 %all-to-all-start.4 = ((bf16[16,32,1024]{2,0,1:T(8,128)(2,1)}), bf16[16,32,1024]{2,0,1:T(8,128)(2,1)}, u32[]{:S(2)}, u32[]{:S(2)}) async-start(bf16[16,32,1024]{2,0,1:T(8,128)(2,1)} %copy.37), calls=%async_computation.4 | async-start | bytes 2097152 | tf_op jit(solution)/shard_map/all_to_all | solution.py:124
  181.0 0.1 iota_compare_fusion.2
  181.2 0.2 eq.81
  181.3 55.9 %all-to-all-done.4 = bf16[16,32,1024]{2,0,1:T(8,128)(2,1)} async-done(((bf16[16,32,1024]{2,0,1:T(8,128)(2,1)}), bf16[16,32,1024]{2,0,1:T(8,128)(2,1)}, u32[]{:S(2)}, u32[]{:S(2)}) %all-to-all-start.4) | async-done | bytes 1048608 | tf_op jit(solution)/shard_map/all_to_all | solution.py:124
  237.2 1.8 copy.38
  239.0 0.0 copy-done.6
  239.0 0.4 fusion.32
  239.5 0.8 fusion.79
  (11 shorter events, 0.1 us)
Async XLA Ops:
  6.5 59.7 %copy-start = (bf16[1024,1024]{1,0:T(8,128)(2,1)S(1)}, bf16[1024,1024]{1,0:T(8,128)(2,1)}, u32[]{:S(2)}) copy-start(bf16[1024,1024]{1,0:T(8,128)(2,1)} %param.21) | copy-start | bytes 6291460
  6.5 11.7 %copy-start.5 = (s32[1,128,2]{1,2,0:T(2,128)S(1)}, s32[1,128,2]{1,2,0:T(2,128)}, u32[]{:S(2)}) copy-start(s32[1,128,2]{1,2,0:T(2,128)} %param.24) | copy-start | bytes 3076
  12.7 22.2 %all-to-all-start = ((bf16[16,128,256]{1,2,0:T(8,128)(2,1)}), bf16[16,128,256]{1,2,0:T(8,128)(2,1)}, u32[]{:S(2)}, u32[]{:S(2)}) async-start(bf16[16,128,256]{1,2,0:T(8,128)(2,1)} %fusion.60), calls=%async_computation | async-start | bytes 2097152 | tf_op jit(solution)/shard_map/all_to_all | solution.py:77
  46.7 13.3 %copy-start.2 = (bf16[1,64,1024]{2,1,0:T(8,128)(2,1)S(1)}, bf16[1,64,1024]{2,1,0:T(8,128)(2,1)}, u32[]{:S(2)}) copy-start(bf16[1,64,1024]{2,1,0:T(8,128)(2,1)} %param.27) | copy-start | bytes 393220
  47.7 18.6 %copy-start.3 = (f32[1,2,1024]{2,1,0:T(2,128)S(1)}, f32[1,2,1024]{2,1,0:T(2,128)}, u32[]{:S(2)}) copy-start(f32[1,2,1024]{2,1,0:T(2,128)} %param.23) | copy-start | bytes 24580
  47.7 18.6 %copy-start.4 = (f32[1,2,1024]{2,1,0:T(2,128)S(1)}, f32[1,2,1024]{2,1,0:T(2,128)}, u32[]{:S(2)}) copy-start(f32[1,2,1024]{2,1,0:T(2,128)} %param.22) | copy-start | bytes 24580
  47.7 18.6 %copy-start.1 = (bf16[1,128,1024]{2,1,0:T(8,128)(2,1)S(1)}, bf16[1,128,1024]{2,1,0:T(8,128)(2,1)}, u32[]{:S(2)}) copy-start(bf16[1,128,1024]{2,1,0:T(8,128)(2,1)} %param.15) | copy-start | bytes 786436
  48.5 11.6 %all-to-all-start.1 = ((bf16[16,128,64]{1,2,0:T(8,128)(2,1)}), bf16[16,128,64]{1,2,0:T(8,128)(2,1)S(1)}, u32[]{:S(2)}, u32[]{:S(2)}) async-start(bf16[16,128,64]{1,2,0:T(8,128)(2,1)} %copy_bitcast_fusion), calls=%async_computation.1 | async-start | bytes 524288 | tf_op jit(solution)/shard_map/all_to_all | solution.py:86
  61.6 32.3 %all-to-all-start.3 = ((bf16[16,1,64,1024]{3,2,1,0:T(8,128)(2,1)}), bf16[16,1,64,1024]{3,2,1,0:T(8,128)(2,1)}, u32[]{:S(2)}, u32[]{:S(2)}) async-start(bf16[16,1,64,1024]{3,2,1,0:T(8,128)(2,1)} %stack.2), calls=%async_computation.3 | async-start | bytes 4194304 | tf_op jit(solution)/shard_map/all_to_all | solution.py:57
  93.9 73.6 %all-to-all-start.2 = ((bf16[16,32,1024]{2,0,1:T(8,128)(2,1)}), bf16[16,32,1024]{2,0,1:T(8,128)(2,1)}, u32[]{:S(2)}, u32[]{:S(2)}) async-start(bf16[16,32,1024]{2,0,1:T(8,128)(2,1)} %copy.34), calls=%async_computation.2 | async-start | bytes 2097152 | tf_op jit(solution)/shard_map/all_to_all | solution.py:113
  111.5 44.7 %all-gather.2.cloned.1.call-start = ((), (), s32[]{:S(2)}) async-start(), calls=%async_computation.5 | async-start | bytes 2228224 | tf_op jit(solution)/shard_map/all_gather | solution.py:55
  173.7 65.3 %copy-start.6 = (f32[1,128,2]{1,2,0:T(2,128)S(1)}, f32[1,128,2]{1,2,0:T(2,128)}, u32[]{:S(2)}) copy-start(f32[1,128,2]{1,2,0:T(2,128)} %param.25) | copy-start | bytes 3076
  176.5 60.6 %all-to-all-start.4 = ((bf16[16,32,1024]{2,0,1:T(8,128)(2,1)}), bf16[16,32,1024]{2,0,1:T(8,128)(2,1)}, u32[]{:S(2)}, u32[]{:S(2)}) async-start(bf16[16,32,1024]{2,0,1:T(8,128)(2,1)} %copy.37), calls=%async_computation.4 | async-start | bytes 2097152 | tf_op jit(solution)/shard_map/all_to_all | solution.py:124
Sparse Core Ops, SparseCore 0:
  114.5 41.6 all-gather.1
